TPU v7x, 1024 devices: a whole 8x8x8 slice. The times are simulated.
1024 devices in a mesh: row: 32 (over y_lo, z, core), col: 32 (over x, y_hi).
Axes of the slice: x: 8, y: 8 (y_hi: 4, y_lo: 2; y = y_hi * 2 + y_lo), z: 8, core: 2. Of those that a mesh axis runs over, the one named last changes fastest.
Arguments:
- tiles: bfloat16 [32, 32, 6, 256, 256], P('row', 'col'), may hold values from -0.25 to 0.25
- tile_rows: int32 [32, 32, 6], P('row', 'col'), may hold values from 0 to 63, as said below
- tile_cols: int32 [32, 32, 6], P('row', 'col'), may hold values from 0 to 63, as said below
- tile_counts: int32 [32, 32], P('row', 'col'), may hold values from 1 to 6, as said below
- trial: float32 [2048, 16, 256], P(('row', 'col'))
- search: float32 [2048, 16, 256], P(('row', 'col'))
Outputs:
- residual: float32 [2048, 16, 256], P(('row', 'col'))
- rayleigh: float32 [16, 16], replicated
- gram: float32 [32, 32], replicated
Inputs may be any that keep to these rules, and one draw needn't show every extreme that they name: `tile_rows`: every slot lies in the lower triangle: the global block row of a slot is at least its global block column. `tile_cols`: lower triangle as stated for tile_rows. `tile_counts`: some device uses all 6 slots.
All inputs are finite; a program needn't handle non-finite values.
Results may differ from a plain program's by a relative error of at most 0.0029.
Values may be sent and summed in bfloat16 or wider, within the bound.
A program may use at most 32 MiB of HBM per device.

v0:
```python
import jax
import jax.numpy as jnp
from jax import lax
from jax.sharding import PartitionSpec as P


def inner_gram(left, right):
    return jnp.einsum("bkt,blt->kl", left, right, precision=lax.Precision.HIGHEST)


def slot_products(tile_data, row_index, col_index, live_slots, row_vecs, col_vecs):
    col_sel = col_vecs[col_index]
    row_sel = row_vecs[row_index]
    by_row = (
        jnp.einsum("sij,skj->ski", tile_data, col_sel, preferred_element_type=jnp.float32)
        * live_slots
    )
    by_col = (
        jnp.einsum("sij,ski->skj", tile_data, row_sel, preferred_element_type=jnp.float32)
        * live_slots
    )
    row_terms = jnp.zeros(row_vecs.shape, jnp.float32).at[row_index].add(by_row)
    col_terms = jnp.zeros(col_vecs.shape, jnp.float32).at[col_index].add(by_col)
    return (row_terms, col_terms)


def local(tiles, tile_rows, tile_cols, tile_counts, trial, search):
    tile_data = tiles[0, 0]
    row_index = tile_rows[0, 0]
    col_index = tile_cols[0, 0]
    used_count = tile_counts[0, 0]
    slot_total = tile_data.shape[0]
    live_slots = (jnp.arange(slot_total, dtype=jnp.int32) < used_count).astype(jnp.float32)[
        :, None, None
    ]
    basis_size = trial.shape[0] * trial.shape[2] * lax.axis_size("row") * lax.axis_size("col")
    trial_low = trial.astype(jnp.bfloat16)
    col_vecs = lax.all_gather(trial_low, "row", axis=0, tiled=True)
    row_vecs = lax.all_gather(trial_low, "col", axis=0, tiled=True)
    row_terms, col_terms = slot_products(
        tile_data, row_index, col_index, live_slots, row_vecs, col_vecs
    )
    image = lax.psum_scatter(row_terms, "col", scatter_dimension=0, tiled=True) + lax.psum_scatter(
        col_terms, "row", scatter_dimension=0, tiled=True
    )
    correlation_sum, projected_sum = lax.psum(
        (inner_gram(trial, trial), inner_gram(trial, image)), ("row", "col")
    )
    correlation = correlation_sum / basis_size
    projected = projected_sum / basis_size
    factor = jnp.linalg.cholesky(correlation)
    rayleigh = jax.scipy.linalg.cho_solve((factor, True), projected)
    residual = image - jnp.einsum("bkt,kl->blt", trial, rayleigh, precision=lax.Precision.HIGHEST)
    res_sum, mixed_sum, search_sum = lax.psum(
        (inner_gram(residual, residual), inner_gram(residual, search), inner_gram(search, search)),
        ("row", "col"),
    )
    res_res = res_sum / basis_size
    res_search = mixed_sum / basis_size
    search_search = search_sum / basis_size
    upper = jnp.concatenate([res_res, res_search], axis=1)
    lower = jnp.concatenate([res_search.T, search_search], axis=1)
    gram = jnp.concatenate([upper, lower], axis=0)
    return (residual, rayleigh, gram)


def solution(mesh):
    return jax.shard_map(
        local,
        mesh=mesh,
        in_specs=(
            P("row", "col", None, None, None),
            P("row", "col", None),
            P("row", "col", None),
            P("row", "col"),
            P(("row", "col"), None, None),
            P(("row", "col"), None, None),
        ),
        out_specs=(P(("row", "col"), None, None), P(), P()),
        check_vma=False,
    )
```

profile of v0, /device:TPU:1, one launch (start us, length us, event | category | flops | bytes accessed | tf_op | source)
XLA Modules:
  0.0 654.3 jit_solution(13036742918899491816)
XLA Ops:
  7.2 0.8 convert_element_type.10
  8.1 49.7 %all_gather.6 = bf16[64,16,256]{2,1,0:T(8,128)(2,1)S(1)} all-gather(bf16[2,16,256]{2,1,0:T(8,128)(2,1)S(1)} %convert_element_type.10), channel_id=1, replica_groups=mesh['row'=32,'col'=32] {'row'}, dimensions={0}, use_global_device_ids=true | all-gather | bytes 540672 | tf_op jit(solution)/shard_map/all_gather | solution.py:38
  58.5 0.6 copy-done.8
  59.1 0.5 gather_fusion
  59.7 0.3 convolution_multiply_fusion.1
  60.1 0.8 scatter_fusion
  60.9 1.0 copy-done.2
  62.0 71.0 %all_gather.7 = bf16[64,16,256]{2,1,0:T(8,128)(2,1)S(1)} all-gather(bf16[2,16,256]{2,1,0:T(8,128)(2,1)S(1)} %convert_element_type.10), channel_id=1, replica_groups=mesh['row'=32,'col'=32] {'col'}, dimensions={0}, use_global_device_ids=true | all-gather | bytes 540672 | tf_op jit(solution)/shard_map/all_gather | solution.py:39
  133.0 0.5 gather_fusion.1
  133.9 0.8 scatter_fusion.1
  134.7 1.0 copy-done.1
  135.9 0.6 copy-done.5
  136.7 149.5 %reduce-scatter.3.cloned.1.call-done = f32[2,16,256]{2,1,0:T(8,128)} async-done(((f32[64,16,256]{2,1,0:T(8,128)}), f32[2,16,256]{2,1,0:T(8,128)}) %reduce-scatter.3.cloned.1.call-update) | async-done | bytes 32784 | tf_op jit(solution)/shard_map/reduce_scatter | solution.py:43
  286.2 128.2 %reduce-scatter.5.cloned.1.call-done = f32[2,16,256]{2,1,0:T(8,128)} async-done(((f32[64,16,256]{2,1,0:T(8,128)}), f32[2,16,256]{2,1,0:T(8,128)}) %reduce-scatter.5.cloned.1.call-update) | async-done | bytes 32784 | tf_op jit(solution)/shard_map/reduce_scatter | solution.py:43
  414.4 0.8 add.60
  415.3 115.5 %all-reduce.1 = (f32[16,16]{0,1:T(8,128)S(1)}, f32[16,16]{0,1:T(8,128)S(1)}) all-reduce(f32[16,16]{0,1:T(8,128)S(1)} %convolution_bitcast_fusion.5, f32[16,16]{0,1:T(8,128)S(1)} %convolution_bitcast_fusion.4), channel_id=1, replica_groups=mesh['row'=32,'col'=32] {'row','col'}, use_global_device_ids=true, to_apply=%region_4.0 | all-reduce | flops 512 | bytes 4096 | tf_op jit(solution)/shard_map/psum | solution.py:46
  530.9 1.5 cholesky.16
  532.4 0.6 compare_reduce_fusion
  533.0 0.6 fusion.3
  533.7 1.2 custom-call.10
  535.5 0.4 copy-done.6
  536.0 0.5 copy-done.4
  536.6 110.0 %all-reduce = (f32[16,16]{0,1:T(8,128)S(1)}, f32[16,16]{0,1:T(8,128)S(1)}, f32[16,16]{0,1:T(8,128)S(1)}) all-reduce(f32[16,16]{0,1:T(8,128)S(1)} %convolution_bitcast_fusion.1, f32[16,16]{0,1:T(8,128)S(1)} %convolution_bitcast_fusion.2, f32[16,16]{0,1:T(8,128)S(1)} %convolution_bitcast_fusion.3), channel_id=1, replica_groups=mesh['row'=32,'col'=32] {'row','col'}, use_global_device_ids=true, to_apply=%region_10.11 | all-reduce | flops 768 | bytes 6144 | tf_op jit(solution)/shard_map/psum | solution.py:54
  646.8 0.7 copy.24
  (40 shorter events, 2.2 us)
Async XLA Ops:
  7.2 52.5 %copy-start = (bf16[1,1,6,256,256]{4,3,2,1,0:T(8,128)(2,1)S(1)}, bf16[1,1,6,256,256]{4,3,2,1,0:T(8,128)(2,1)}, u32[]{:S(2)}) copy-start(bf16[1,1,6,256,256]{4,3,2,1,0:T(8,128)(2,1)} %param.6) | copy-start | bytes 2359300
  7.2 279.0 %reduce-scatter.3.cloned.1.call-start = ((), (), s32[]{:S(2)}) async-start(), calls=%async_computation.2 | async-start | bytes 1081344 | tf_op jit(solution)/shard_map/reduce_scatter | solution.py:43
  8.1 49.7 %copy-start.7 = (s32[1,1,6]{2,1,0:T(1,128)S(1)}, s32[1,1,6]{2,1,0:T(1,128)}, u32[]{:S(2)}) copy-start(s32[1,1,6]{2,1,0:T(1,128)} %param.8) | copy-start | bytes 76
  58.5 0.7 copy-start.8
  60.9 1.0 copy-start.2
  61.9 352.4 %reduce-scatter.5.cloned.1.call-start = ((), (), s32[]{:S(2)}) async-start(), calls=%async_computation.3 | async-start | bytes 1081344 | tf_op jit(solution)/shard_map/reduce_scatter | solution.py:43
  134.7 1.0 copy-start.1
  134.7 1.1 copy-start.3
  135.7 0.8 copy-start.5
  535.3 0.6 copy-start.6
  535.9 0.6 copy-start.4
Sparse Core Ops, SparseCore 0:
  62.0 224.0 reduce-scatter.2
  289.5 124.7 reduce-scatter.4
where the time goes:
time: 655 us; the launch traced here: 654 us
  blocking collectives  346 us (53%)
  waiting for transfers between devices  278 us (42%)
  between operations  14.9 us (2%)
  other arithmetic  7.28 us (1%)
    reduce_scatter x1, waiting for transfers between devices, local(): lax.psum_scatter(row_terms, 'col', scatter_dimension=0, tiled=True)  150 us
    reduce_scatter x1, waiting for transfers between devices, local(): lax.psum_scatter(col_terms, 'row', scatter_dimension=0, tiled=True)  128 us
    psum x1, blocking collectives, local(): lax.psum((inner_gram(trial, trial), inner_gram(trial, image)), ('row', 'c...  116 us
    psum x1, blocking collectives, local(): lax.psum((inner_gram(residual, residual), inner_gram(residual, search), i...  110 us
    all_gather x1, blocking collectives, local(): row_vecs = lax.all_gather(trial_low, 'col', axis=0, tiled=True)  71 us
    all_gather x1, blocking collectives, local(): col_vecs = lax.all_gather(trial_low, 'row', axis=0, tiled=True)  49.7 us
  transfers between devices with their start and end apart: 2, of which 2 were waited for; matrix products, arithmetic and copies ran while one was open for 0% of the time, Pallas kernels for 0%

commit v1 on v0

v1 whole, which is shorter than its diff:
```python
import jax
import jax.numpy as jnp
from jax import lax
from jax.experimental import pallas as pl
from jax.experimental.pallas import tpu as pltpu
from jax.sharding import PartitionSpec as P

MESH = pl.DeviceIdType.MESH
HI = lax.Precision.HIGHEST
F32 = jnp.float32
BF16 = jnp.bfloat16
SLOTS = 6
STATES = 16
TILE = 256
NT = (((1,), (1,)), ((), ()))
NN = (((1,), (0,)), ((), ()))


class Sems:
    def __init__(self, send, recv):
        self.send, self.recv, self.used, self.copies = send, recv, 0, []

    def copy(self, src, dst, peer):
        at = self.used
        self.used += 1
        c = pltpu.make_async_remote_copy(
            src_ref=src, dst_ref=dst, send_sem=self.send.at[at], recv_sem=self.recv.at[at],
            device_id=peer, device_id_type=MESH)
        c.start()
        self.copies.append(c)
        return c


class Ring:
    def __init__(self, sems, at, peer, far_up):
        self.sems, self.at, self.peer, self.far_up = sems, at, peer, far_up

    def first(self):
        own = self.at(0)
        self.c = {d: self.sems.copy(own, own, self.peer(d)) for d in (2, -2, 1, -1)}

    def second(self):
        for sign in (1, -1):
            self.c[2 * sign].wait_recv()
            src = self.at(-2 * sign)
            if (sign > 0) == self.far_up:
                self.c[4] = self.sems.copy(src, src, self.peer(2 * sign))
            self.c[3 * sign] = self.sems.copy(src, src, self.peer(sign))

    def last(self):
        for d in (1, -1, 3, -3, 4):
            self.c[d].wait_recv()


def kernel(tiles, rows, cols, count, trial, search, residual, rayleigh, gram,
           tile_buf, gath_r, gath_c, con_r, con_c, code_r, code_c, acc_r, acc_c, part_r, part_c,
           ar1x, ar1h, ar1l, ar1z, ar2x, ar2h, ar2l, ar2z, pack, tile_sem, send, recv):
    p, q = lax.axis_index("row"), lax.axis_index("col")
    x, yh = q // 4, q % 4
    yl, z, core = p // 16, (p // 2) % 8, p % 2
    al = yl * 2 + core
    sems = Sems(send, recv)

    def x_peer(d):
        return (p, ((x + d + 8) % 8) * 4 + yh)

    def h_peer(d):
        return (p, x * 4 + (yh + d) % 4)

    def z_peer(d):
        return (yl * 16 + ((z + d + 8) % 8) * 2 + core, q)

    def l_peer(d):
        a = (al + d) % 4
        return ((a // 2) * 16 + z * 2 + a % 2, q)

    fetch = pltpu.make_async_copy(tiles.at[0, 0], tile_buf, tile_sem)
    fetch.start()

    barrier = pltpu.get_barrier_semaphore()
    for d in range(1, 8):
        for peer in (x_peer(d), z_peer(d)):
            pl.semaphore_signal(barrier, inc=1, device_id=peer, device_id_type=MESH)
    for d in range(1, 4):
        for peer in (h_peer(d), l_peer(d)):
            pl.semaphore_signal(barrier, inc=1, device_id=peer, device_id_type=MESH)

    used = count[0, 0]
    row_at, col_at, live = [], [], []
    for s in range(SLOTS):
        i, j = rows[0, 0, s], cols[0, 0, s]
        row_at.append(i)
        col_at.append(((j // 4) % 8) * 8 + (j // 32) * 4 + j % 4)
        live.append(jnp.where(s < used, 1.0, 0.0).astype(F32))

    low = trial[...].astype(BF16)
    own_r = pl.ds(pl.multiple_of(x * 8 + yh * 2, 2), 2)
    own_c = pl.ds(pl.multiple_of(z * 8 + al * 2, 2), 2)
    gath_r[own_r] = low
    gath_c[own_c] = low

    lane = lax.broadcasted_iota(jnp.int32, (8, 128), 1)
    for at, code, me in ((row_at, code_r, x), (col_at, code_c, z)):
        value = jnp.full((8, 128), -1.0, F32)
        for s in range(SLOTS):
            target = (at[s] * 16 + lane % 16).astype(F32)
            value = jnp.where(lane // 16 == s, target * live[s] - (1.0 - live[s]), value)
        code[me] = value
    pad = jnp.zeros((8, 32, TILE), BF16)
    con_r[:, 96:, :] = pad
    con_c[:, 96:, :] = pad
    pack[...] = jnp.zeros(pack.shape, F32)

    trial_cat = jnp.concatenate([trial[0], trial[1]], axis=1)
    search_cat = jnp.concatenate([search[0], search[1]], axis=1)
    corr = lax.dot_general(trial_cat, trial_cat, NT, precision=HI, preferred_element_type=F32)

    pl.semaphore_wait(barrier, 20)

    def ring_of(buf, base, me_b, me_a, peer, d):
        def at(off):
            return buf.at[pl.ds(((me_b + off + 8) % 8) * 8 + ((me_a - d + 4) % 4) * 2, 2)]
        return Ring(sems, at, peer, d < 2)

    rings_r = [ring_of(gath_r, 0, x, yh, x_peer, d) for d in range(4)]
    rings_c = [ring_of(gath_c, 0, z, al, z_peer, d) for d in range(4)]
    group_c = {d: sems.copy(gath_c.at[own_c], gath_c.at[own_c], l_peer(d)) for d in (1, 2, 3)}
    group_r = {d: sems.copy(gath_r.at[own_r], gath_r.at[own_r], h_peer(d)) for d in (2, 1, 3)}
    rings_r[0].first()
    rings_c[0].first()
    for d in (1, 2, 3):
        group_c[d].wait_recv()
        rings_c[d].first()
    for d in (1, 3):
        group_r[d].wait_recv()
        rings_r[d].first()
    rings_r[0].second()
    rings_c[0].second()
    group_r[2].wait_recv()
    rings_r[2].first()
    for d in (1, 3, 2):
        rings_c[d].second()
        rings_r[d].second()
    codes = []
    for d in range(1, 8):
        codes.append(sems.copy(code_r.at[x], code_r.at[x], x_peer(d)))
        codes.append(sems.copy(code_c.at[z], code_c.at[z], z_peer(d)))
    fetch.wait()
    for d in (0, 1, 3, 2):
        rings_c[d].last()
        rings_r[d].last()

    def con_ring(buf, me, peer, half):
        def at(off):
            return buf.at[(me + off + 8) % 8, pl.ds(half * 48, 48)]
        return Ring(sems, at, peer, half == 0)

    out_r = [con_ring(con_r, x, x_peer, h) for h in range(2)]
    out_c = [con_ring(con_c, z, z_peer, h) for h in range(2)]
    row_sel = [gath_r[row_at[s]] for s in range(SLOTS)]
    by_row = []
    for s in range(SLOTS):
        col_sel = gath_c[col_at[s]]
        product = lax.dot_general(col_sel, tile_buf[s], NT, preferred_element_type=F32) * live[s]
        by_row.append(product)
        con_r[x, pl.ds(s * 16, 16), :] = product.astype(BF16)

    def group_start(buf, me, peer, value, n):
        buf[me] = value
        own = buf.at[me]
        return [sems.copy(own, own, peer(d)) for d in range(1, n)]

    def group_sum(buf, copies, n):
        for c in copies:
            c.wait_recv()
        total = buf[0]
        for i in range(1, n):
            total = total + buf[i]
        return total

    left = jnp.concatenate([v.astype(F32) for v in row_sel], axis=1)
    right = jnp.concatenate(by_row, axis=1)
    mixed = lax.dot_general(left, right, NT, precision=HI, preferred_element_type=F32)
    pack[0:16, 0:16] = corr
    pack[16:32, 0:16] = mixed
    both = (pack[0:8] + pltpu.roll(pack[8:16], 32, 1) + pltpu.roll(pack[16:24], 64, 1)
            + pltpu.roll(pack[24:32], 96, 1))
    first_x = group_start(ar1x, x, x_peer, both, 8)
    out_r[0].first()
    out_r[1].first()

    for s in range(SLOTS):
        product = lax.dot_general(row_sel[s], tile_buf[s], NN, preferred_element_type=F32) * live[s]
        con_c[z, pl.ds(s * 16, 16), :] = product.astype(BF16)
    out_c[0].first()
    out_c[1].first()

    first_h = group_start(ar1h, yh, h_peer, group_sum(ar1x, first_x, 8), 4)
    for ring in (out_r[0], out_c[0], out_r[1], out_c[1]):
        ring.second()
    first_l = group_start(ar1l, al, l_peer, group_sum(ar1h, first_h, 4), 4)
    first_z = group_start(ar1z, z, z_peer, group_sum(ar1l, first_l, 4), 8)

    for c in codes:
        c.wait_recv()
    sub = lax.broadcasted_iota(jnp.int32, (128, 128), 0)

    def reduce_first(buf, code, rings, me_b, me_a, acc, part, peer):
        for ring in rings:
            ring.last()
        base = (sub + me_b * 128).astype(F32)
        total = jnp.zeros((128, TILE), F32)
        for b in range(8):
            pick = jnp.where(code[b][0:1, :] == base, 1.0, 0.0).astype(BF16)
            total = total + lax.dot_general(pick, buf[b], NN, preferred_element_type=F32)
        acc[...] = total.reshape(4, 32, TILE)
        return [sems.copy(acc.at[(me_a + d) % 4], part.at[d - 1], peer(d)) for d in (2, 1, 3)]

    parts = reduce_first(con_r, code_r, out_r, x, yh, acc_r, part_r, h_peer)
    parts = parts + reduce_first(con_c, code_c, out_c, z, al, acc_c, part_c, l_peer)

    total = group_sum(ar1z, first_z, 8) / BASIS
    corr = jnp.concatenate([total, pltpu.roll(total, 96, 1)], axis=0)
    mixed = jnp.concatenate([pltpu.roll(total, 64, 1), pltpu.roll(total, 32, 1)], axis=0)
    ident = (lax.broadcasted_iota(jnp.int32, (16, 16), 0)
             == lax.broadcasted_iota(jnp.int32, (16, 16), 1)).astype(F32)
    flip = lax.dot_general(ident, mixed[:, 0:16], NT, precision=HI, preferred_element_type=F32)
    pack[0:16, 0:16] = corr[:, 0:16]
    pack[0:16, 16:32] = mixed[:, 0:16] + flip
    work = pack[0:16, :]
    row_id = lax.broadcasted_iota(jnp.int32, (16, 128), 0)
    for j in range(STATES):
        pivot = work[j:j + 1, :] / work[j:j + 1, j:j + 1]
        work = jnp.where(row_id == j, pivot, work - work[:, j:j + 1] * pivot)
    pack[0:16, :] = work
    quotient = pack[0:16, 16:32]
    rayleigh[...] = quotient
    turned = lax.dot_general(ident, quotient, NT, precision=HI, preferred_element_type=F32)

    for c in parts:
        c.wait_recv()
    image = (acc_r[yh] + part_r[0] + part_r[1] + part_r[2]
             + acc_c[al] + part_c[0] + part_c[1] + part_c[2])
    fixed = lax.dot_general(turned, trial_cat, NN, precision=HI, preferred_element_type=F32)
    res0 = image[0:16] - fixed[:, 0:TILE]
    res1 = image[16:32] - fixed[:, TILE:]
    residual[0] = res0
    residual[1] = res1
    stack = jnp.concatenate([jnp.concatenate([res0, res1], axis=1), search_cat], axis=0)
    local = lax.dot_general(stack, stack, NT, precision=HI, preferred_element_type=F32)
    pack[...] = jnp.zeros(pack.shape, F32)
    pack[:, 0:32] = local
    both = (pack[0:8] + pltpu.roll(pack[8:16], 32, 1) + pltpu.roll(pack[16:24], 64, 1)
            + pltpu.roll(pack[24:32], 96, 1))
    step = group_start(ar2x, x, x_peer, both, 8)
    step = group_start(ar2h, yh, h_peer, group_sum(ar2x, step, 8), 4)
    step = group_start(ar2l, al, l_peer, group_sum(ar2h, step, 4), 4)
    step = group_start(ar2z, z, z_peer, group_sum(ar2l, step, 4), 8)
    total = group_sum(ar2z, step, 8) / BASIS
    for g in range(4):
        spread = total if g == 0 else pltpu.roll(total, 128 - 32 * g, 1)
        gram[8 * g:8 * g + 8, :] = spread[:, 0:32]

    for c in sems.copies:
        c.wait_send()


BASIS = 524288.0
COPIES = 150


def local(tiles, tile_rows, tile_cols, tile_counts, trial, search):
    smem = pl.BlockSpec(memory_space=pltpu.SMEM)
    vmem = pl.BlockSpec(memory_space=pltpu.VMEM)
    return pl.pallas_call(
        kernel,
        out_shape=(
            jax.ShapeDtypeStruct((2, STATES, TILE), F32),
            jax.ShapeDtypeStruct((STATES, STATES), F32),
            jax.ShapeDtypeStruct((2 * STATES, 2 * STATES), F32),
        ),
        in_specs=[pl.BlockSpec(memory_space=pl.ANY), smem, smem, smem, vmem, vmem],
        out_specs=(vmem, vmem, vmem),
        scratch_shapes=[
            pltpu.VMEM((SLOTS, TILE, TILE), BF16),
            pltpu.VMEM((64, STATES, TILE), BF16),
            pltpu.VMEM((64, STATES, TILE), BF16),
            pltpu.VMEM((8, 128, TILE), BF16),
            pltpu.VMEM((8, 128, TILE), BF16),
            pltpu.VMEM((8, 8, 128), F32),
            pltpu.VMEM((8, 8, 128), F32),
            pltpu.VMEM((4, 32, TILE), F32),
            pltpu.VMEM((4, 32, TILE), F32),
            pltpu.VMEM((3, 32, TILE), F32),
            pltpu.VMEM((3, 32, TILE), F32),
        ] + [pltpu.VMEM((n, 8, 128), F32) for n in (8, 4, 4, 8, 8, 4, 4, 8)] + [
            pltpu.VMEM((32, 128), F32),
            pltpu.SemaphoreType.DMA,
            pltpu.SemaphoreType.DMA((COPIES,)),
            pltpu.SemaphoreType.DMA((COPIES,)),
        ],
        compiler_params=pltpu.CompilerParams(collective_id=0, has_side_effects=True),
    )(tiles, tile_rows, tile_cols, tile_counts, trial, search)


def solution(mesh):
    return jax.shard_map(
        local,
        mesh=mesh,
        in_specs=(
            P("row", "col", None, None, None),
            P("row", "col", None),
            P("row", "col", None),
            P("row", "col"),
            P(("row", "col"), None, None),
            P(("row", "col"), None, None),
        ),
        out_specs=(P(("row", "col"), None, None), P(), P()),
        check_vma=False,
    )
```

time: 655 us -> 81.9 us (0.13)
  blocking collectives: 346 us -> 0 us
  waiting for transfers between devices: 278 us -> 0 us
  Pallas kernels: 0 us -> 77.6 us
  between operations: 14.9 us -> 1.3 us
  other arithmetic: 7.28 us -> 0 us
    reduce_scatter x2 -> x0, waiting for transfers between devices: 278 us -> none  [the longest x1 150 us: local(): lax.psum_scatter(row_terms, 'col', scatter_dimension=0, tiled=True)]
    psum x2 -> x0, blocking collectives: 226 us -> none  [the longest x1 116 us: local(): lax.psum((inner_gram(trial, trial), inner_gram(trial, image)), ('row', 'c...]
    all_gather x2 -> x0, blocking collectives: 121 us -> none  [the longest x1 71 us: local(): row_vecs = lax.all_gather(trial_low, 'col', axis=0, tiled=True)]
    pallas_call x0 -> x1, Pallas kernels: none -> 77.6 us  [local(): pl.pallas_call(kernel, out_shape=(jax.ShapeDtypeStruct((2, STATES, TILE),...]
  transfers between devices with their start and end apart: 2 -> 0, of which waited for: 2 -> 0; matrix products, arithmetic and copies ran while one was open for 0% -> 0% of each run, Pallas kernels for 0% -> 0%
where the time goes in v1:
time: 81.9 us; the launch traced here: 81.6 us
  Pallas kernels  77.6 us (95%)
  local copies, waits for them, and re-layouts  2.71 us (3%)
  between operations  1.3 us (2%)
    pallas_call x1, Pallas kernels, local(): pl.pallas_call(kernel, out_shape=(jax.ShapeDtypeStruct((2, STATES, TILE),...  77.6 us
    unnamed x7, local copies, waits for them, and re-layouts  2.71 us

profile of v1, /device:TPU:1, one launch (start us, length us, event | category | flops | bytes accessed | tf_op | source)
XLA Modules:
  0.0 81.6 jit_solution(14024102226417071836)
XLA Ops:
  1.3 77.6 %shard_map.85 = (f32[2,16,256]{2,1,0:T(8,128)}, f32[16,16]{1,0:T(8,128)}, f32[32,32]{1,0:T(8,128)}) custom-call(bf16[1,1,6,256,256]{4,3,2,1,0:T(8,128)(2,1)} %tiles.1, s32[1,1,6]{2,1,0:T(1,128)} %rows.1, s32[1,1,6]{2,1,0:T(1,128)} %cols.1, s32[1,1]{1,0:T(1,128)S(6)} %copy.12.count, f32[2,16,256]{2,1,0:T(8,128)} %trial.1, f32[2,16,256]{2,1,0:T(8,128)} %search.1), custom_call_target="tpu_custom_call" | custom-call | tf_op jit(solution)/shard_map/pallas_call | solution.py:275
  78.8 0.0 copy-start.1
  78.9 1.4 %copy.13 = f32[2,16,256]{2,1,0:T(8,128)} copy(f32[2,16,256]{2,1,0:T(8,128)} %get-tuple-element.6) | data formatting | bytes 65536
  80.2 0.0 copy-done.1
  80.2 0.0 copy-start
  80.2 0.6 copy.14
  80.8 0.1 copy-done
  81.0 0.6 copy.15
Async XLA Ops:
  78.8 1.4 %copy-start.1 = (f32[16,16]{1,0:T(8,128)S(1)}, f32[16,16]{1,0:T(8,128)}, u32[]{:S(2)}) copy-start(f32[16,16]{1,0:T(8,128)} %get-tuple-element.7) | copy-start | bytes 3076
  80.2 0.7 copy-start

commit v2 on v1

v2 whole, which is shorter than its diff:
```python
import jax
import jax.numpy as jnp
from jax import lax
from jax.experimental import pallas as pl
from jax.experimental.pallas import tpu as pltpu
from jax.sharding import PartitionSpec as P

MESH = pl.DeviceIdType.MESH
HI = lax.Precision.HIGHEST
F32 = jnp.float32
BF16 = jnp.bfloat16
SLOTS = 6
STATES = 16
TILE = 256
NT = (((1,), (1,)), ((), ()))
NN = (((1,), (0,)), ((), ()))


class Sems:
    def __init__(self, send, recv):
        self.send, self.recv, self.used, self.copies = send, recv, 0, []

    def copy(self, src, dst, peer):
        at = self.used
        self.used += 1
        c = pltpu.make_async_remote_copy(
            src_ref=src, dst_ref=dst, send_sem=self.send.at[at], recv_sem=self.recv.at[at],
            device_id=peer, device_id_type=MESH)
        c.start()
        self.copies.append(c)
        return c


class Ring:
    def __init__(self, sems, at, peer, far_up):
        self.sems, self.at, self.peer, self.far_up = sems, at, peer, far_up

    def first(self):
        own = self.at(0)
        self.c = {d: self.sems.copy(own, own, self.peer(d)) for d in (2, -2, 1, -1)}

    def second(self):
        for sign in (1, -1):
            self.c[2 * sign].wait_recv()
            src = self.at(-2 * sign)
            if (sign > 0) == self.far_up:
                self.c[4] = self.sems.copy(src, src, self.peer(2 * sign))
            self.c[3 * sign] = self.sems.copy(src, src, self.peer(sign))

    def last(self):
        for d in (1, -1, 3, -3, 4):
            self.c[d].wait_recv()


class Direct(Ring):
    def first(self):
        own = self.at(0)
        self.c = {d: self.sems.copy(own, own, self.peer(d)) for d in (4, 3, -3, 2, -2, 1, -1)}

    def second(self):
        pass

    def last(self):
        for d in (1, -1, 2, -2, 3, -3, 4):
            self.c[d].wait_recv()


def pack_rows(buf, rows, shift):
    total = buf[0:8]
    for i in range(1, rows // 8):
        total = total + pltpu.roll(buf[8 * i:8 * i + 8], shift * i, 1)
    return total


def kernel(tiles, rows, cols, count, trial, search, residual, rayleigh, gram,
           tile_buf, gath_r, gath_c, con_r, con_c, code_r, code_c, acc_r, acc_c, low_r, low_c, part_r, part_c,
           ar0x, ar0y, ar0z, ar1x, ar1y, ar1z, pack, known, tile_sem, send, recv):
    p, q = lax.axis_index("row"), lax.axis_index("col")
    x, yh = q // 4, q % 4
    yl, z, core = p // 16, (p // 2) % 8, p % 2
    al = yl * 2 + core
    yc = (yh * 2 + yl) * 2 + core
    sems = Sems(send, recv)

    def x_peer(d):
        return (p, ((x + d + 8) % 8) * 4 + yh)

    def h_peer(d):
        return (p, x * 4 + (yh + d) % 4)

    def z_peer(d):
        return (yl * 16 + ((z + d + 8) % 8) * 2 + core, q)

    def l_peer(d):
        a = (al + d) % 4
        return ((a // 2) * 16 + z * 2 + a % 2, q)

    def y_peer(d):
        a = (yc + d) % 16
        return (((a // 2) % 2) * 16 + z * 2 + a % 2, x * 4 + a // 4)

    ring_order = (4, 3, 5, 2, 6, 1, 7)
    y_order = (8, 9, 7, 6, 10, 11, 5, 4, 12, 13, 3, 2, 14, 15, 1)

    barrier = pltpu.get_barrier_semaphore()
    for peer in [x_peer(d) for d in ring_order] + [z_peer(d) for d in ring_order] + [y_peer(d) for d in y_order]:
        pl.semaphore_signal(barrier, inc=1, device_id=peer, device_id_type=MESH)
    fetch = pltpu.make_async_copy(tiles.at[0, 0], tile_buf, tile_sem)
    fetch.start()

    low = trial[...].astype(BF16)
    own_r = pl.ds(pl.multiple_of(x * 8 + yh * 2, 2), 2)
    own_c = pl.ds(pl.multiple_of(z * 8 + al * 2, 2), 2)
    gath_r[own_r] = low
    gath_c[own_c] = low

    trial_cat = jnp.concatenate([trial[0], trial[1]], axis=1)
    search_cat = jnp.concatenate([search[0], search[1]], axis=1)
    held = jnp.concatenate([trial_cat, search_cat], axis=0)
    pack[...] = jnp.zeros(pack.shape, F32)
    pack[:, 0:32] = lax.dot_general(held, held, NT, precision=HI, preferred_element_type=F32)

    pl.semaphore_wait(barrier, 29)

    def group_start(buf, me, peer, order, value):
        buf[me] = value
        own = buf.at[me]
        return [sems.copy(own, own, peer(d)) for d in order]

    def group_sum(buf, copies, n):
        for c in copies:
            c.wait_recv()
        total = buf[0]
        for i in range(1, n):
            total = total + buf[i]
        return total

    def ring_of(kind, buf, me_b, me_a, peer, d):
        def at(off):
            return buf.at[pl.ds(((me_b + off + 8) % 8) * 8 + ((me_a - d + 4) % 4) * 2, 2)]
        return kind(sems, at, peer, d < 2)

    rings_r = [ring_of(Direct if d == 2 else Ring, gath_r, x, yh, x_peer, d) for d in range(4)]
    rings_c = [ring_of(Ring, gath_c, z, al, z_peer, d) for d in range(4)]
    group_r = {d: sems.copy(gath_r.at[own_r], gath_r.at[own_r], h_peer(d)) for d in (2, 1, 3)}
    rings_r[0].first()
    group_c = {d: sems.copy(gath_c.at[own_c], gath_c.at[own_c], l_peer(d)) for d in (2, 1, 3)}
    rings_c[0].first()

    used = count[...]
    row_at, col_at, live = [], [], []
    for s in range(SLOTS):
        i, j = rows[0, 0, s], cols[0, 0, s]
        row_at.append(i)
        col_at.append(((j // 4) % 8) * 8 + (j // 32) * 4 + j % 4)
        live.append(jnp.where(s < used, 1.0, 0.0).astype(F32))
    lane = lax.broadcasted_iota(jnp.int32, (8, 128), 1)
    for at, code, me in ((row_at, code_r, x), (col_at, code_c, z)):
        value = jnp.full((8, 128), -1.0, F32)
        for s in range(SLOTS):
            target = (at[s] * 16 + lane % 16).astype(F32)
            value = jnp.where(lane // 16 == s, target * live[s] - (1.0 - live[s]), value)
        code[me] = value

    codes = []
    for d in ring_order:
        codes.append(sems.copy(code_r.at[x], code_r.at[x], x_peer(d)))
        codes.append(sems.copy(code_c.at[z], code_c.at[z], z_peer(d)))

    for d in (1, 2, 3):
        group_c[d].wait_recv()
        rings_c[d].first()
    ar0 = group_start(ar0x, x, x_peer, ring_order, pack_rows(pack, 32, 32))
    for d in (1, 3):
        group_r[d].wait_recv()
        rings_r[d].first()
    rings_r[0].second()
    rings_c[0].second()
    group_r[2].wait_recv()
    rings_r[2].first()
    for d in (1, 2, 3):
        rings_c[d].second()
    for d in (1, 3):
        rings_r[d].second()
    ar0 = group_start(ar0y, yc, y_peer, y_order, group_sum(ar0x, ar0, 8))
    pad = jnp.zeros((8, 32, TILE), BF16)
    con_r[:, 96:, :] = pad
    con_c[:, 96:, :] = pad
    fetch.wait()
    for d in (0, 1, 2, 3):
        rings_c[d].last()
    for d in (0, 1, 3, 2):
        rings_r[d].last()

    def con_ring(buf, me, peer, half):
        def at(off):
            return buf.at[(me + off + 8) % 8, pl.ds(half * 48, 48)]
        return Ring(sems, at, peer, half == 0)

    out_r = [con_ring(con_r, x, x_peer, h) for h in range(2)]
    out_c = [con_ring(con_c, z, z_peer, h) for h in range(2)]
    for s in range(SLOTS):
        product = lax.dot_general(gath_c[col_at[s]], tile_buf[s], NT, preferred_element_type=F32) * live[s]
        con_r[x, pl.ds(s * 16, 16), :] = product.astype(BF16)
        if s % 3 == 2:
            out_r[s // 3].first()
    for s in range(SLOTS):
        product = lax.dot_general(gath_r[row_at[s]], tile_buf[s], NN, preferred_element_type=F32) * live[s]
        con_c[z, pl.ds(s * 16, 16), :] = product.astype(BF16)
        if s % 3 == 2:
            out_c[s // 3].first()
    for ring in (out_r[0], out_r[1], out_c[0], out_c[1]):
        ring.second()
    ar0 = group_start(ar0z, z, z_peer, ring_order, group_sum(ar0y, ar0, 16))
    for c in codes:
        c.wait_recv()

    sub = lax.broadcasted_iota(jnp.int32, (128, 128), 0)

    def reduce_first(buf, code, rings, me_b, me_a, acc, low, part, peer):
        base = (sub + me_b * 128).astype(F32)
        picks = [jnp.where(code[b][0:1, :] == base, 1.0, 0.0).astype(BF16) for b in range(8)]
        for ring in rings:
            ring.last()
        total = jnp.zeros((128, TILE), F32)
        for b in range(0, 8, 2):
            pick = jnp.concatenate(picks[b:b + 2], axis=1)
            total = total + lax.dot_general(
                pick, buf[b:b + 2].reshape(256, TILE), NN, preferred_element_type=F32)
        acc[...] = total.reshape(4, 32, TILE)
        low[...] = total.astype(BF16).reshape(4, 32, TILE)
        return [sems.copy(low.at[(me_a + d) % 4], part.at[d - 1], peer(d)) for d in (2, 1, 3)]

    parts = reduce_first(con_r, code_r, out_r, x, yh, acc_r, low_r, part_r, h_peer)
    parts = parts + reduce_first(con_c, code_c, out_c, z, al, acc_c, low_c, part_c, l_peer)

    total = group_sum(ar0z, ar0, 8) / BASIS
    known[0:16] = jnp.concatenate([total, pltpu.roll(total, 96, 1)], axis=0)
    known[16:32] = jnp.concatenate([pltpu.roll(total, 64, 1), pltpu.roll(total, 32, 1)], axis=0)
    row_id = lax.broadcasted_iota(jnp.int32, (16, 128), 0)
    lane_id = lax.broadcasted_iota(jnp.int32, (16, 128), 1)
    ident = jnp.where(lane_id == row_id, 1.0, 0.0).astype(F32)
    work = jnp.where(lane_id < 16, known[0:16], pltpu.roll(ident, 16, 1))
    for j in range(STATES):
        pivot = work[j:j + 1, :] / work[j:j + 1, j:j + 1]
        work = jnp.where(row_id == j, pivot, work - work[:, j:j + 1] * pivot)
    pack[0:16, :] = work
    inverse = pack[0:16, 16:32]
    gram[16:32, 16:32] = known[16:32, 16:32]
    pack[...] = jnp.zeros(pack.shape, F32)
    for c in parts:
        c.wait_recv()
    image = acc_r[yh] + acc_c[al]
    for i in range(3):
        image = image + part_r[i].astype(F32) + part_c[i].astype(F32)
    image_cat = jnp.concatenate([image[0:16], image[16:32]], axis=1)
    stack = jnp.concatenate([trial_cat, image_cat, search_cat], axis=0)
    pack[0:16, 0:48] = lax.dot_general(image_cat, stack, NT, precision=HI, preferred_element_type=F32)
    step = group_start(ar1x, x, x_peer, ring_order, pack_rows(pack, 16, 64))

    step = group_start(ar1y, yc, y_peer, y_order, group_sum(ar1x, step, 8))
    step = group_start(ar1z, z, z_peer, ring_order, group_sum(ar1y, step, 16))
    total = group_sum(ar1z, step, 8) / BASIS

    pack[0:16, :] = jnp.concatenate([total, pltpu.roll(total, 64, 1)], axis=0)
    mixed = pack[0:16, 0:16]
    turned = lax.dot_general(mixed, inverse, NN, precision=HI, preferred_element_type=F32)
    fixed = lax.dot_general(turned, trial_cat, NN, precision=HI, preferred_element_type=F32)
    residual[0] = image[0:16] - fixed[:, 0:TILE]
    residual[1] = image[16:32] - fixed[:, TILE:]
    rayleigh[...] = lax.dot_general(inverse, mixed, NT, precision=HI, preferred_element_type=F32)
    gram[0:16, 0:16] = pack[0:16, 16:32] - lax.dot_general(
        turned, mixed, NT, precision=HI, preferred_element_type=F32)
    side = pack[0:16, 32:48] - lax.dot_general(
        turned, known[0:16, 16:32], NN, precision=HI, preferred_element_type=F32)
    gram[0:16, 16:32] = side
    gram[16:32, 0:16] = lax.dot_general(
        ident[:, 0:16], side, NT, precision=HI, preferred_element_type=F32)

    for c in sems.copies:
        c.wait_send()


def hand_on(a, b, c, a_out, b_out, c_out):
    a_out[...] = a[...]
    b_out[...] = b[...]
    c_out[...] = c[...]


BASIS = 524288.0
COPIES = 168


def local(tiles, tile_rows, tile_cols, tile_counts, trial, search):
    smem = pl.BlockSpec(memory_space=pltpu.SMEM)
    vmem = pl.BlockSpec(memory_space=pltpu.VMEM)
    results = pl.pallas_call(
        kernel,
        out_shape=(
            jax.ShapeDtypeStruct((2, STATES, TILE), F32),
            jax.ShapeDtypeStruct((STATES, STATES), F32),
            jax.ShapeDtypeStruct((2 * STATES, 2 * STATES), F32),
        ),
        in_specs=[pl.BlockSpec(memory_space=pl.ANY), smem, smem, vmem, vmem, vmem],
        out_specs=(vmem, vmem, vmem),
        scratch_shapes=[
            pltpu.VMEM((SLOTS, TILE, TILE), BF16),
            pltpu.VMEM((64, STATES, TILE), BF16),
            pltpu.VMEM((64, STATES, TILE), BF16),
            pltpu.VMEM((8, 128, TILE), BF16),
            pltpu.VMEM((8, 128, TILE), BF16),
            pltpu.VMEM((8, 8, 128), F32),
            pltpu.VMEM((8, 8, 128), F32),
            pltpu.VMEM((4, 32, TILE), F32),
            pltpu.VMEM((4, 32, TILE), F32),
            pltpu.VMEM((4, 32, TILE), BF16),
            pltpu.VMEM((4, 32, TILE), BF16),
            pltpu.VMEM((3, 32, TILE), BF16),
            pltpu.VMEM((3, 32, TILE), BF16),
        ] + [pltpu.VMEM((n, 8, 128), F32) for n in (8, 16, 8, 8, 16, 8)] + [
            pltpu.VMEM((32, 128), F32),
            pltpu.VMEM((32, 128), F32),
            pltpu.SemaphoreType.DMA,
            pltpu.SemaphoreType.DMA((COPIES,)),
            pltpu.SemaphoreType.DMA((COPIES,)),
        ],
        compiler_params=pltpu.CompilerParams(collective_id=0, has_side_effects=True),
    )(tiles, tile_rows, tile_cols, tile_counts, trial, search)
    return pl.pallas_call(
        hand_on,
        out_shape=tuple(jax.ShapeDtypeStruct(r.shape, F32) for r in results),
        in_specs=[vmem] * 3,
        out_specs=(vmem,) * 3,
    )(*results)


def solution(mesh):
    return jax.shard_map(
        local,
        mesh=mesh,
        in_specs=(
            P("row", "col", None, None, None),
            P("row", "col", None),
            P("row", "col", None),
            P("row", "col"),
            P(("row", "col"), None, None),
            P(("row", "col"), None, None),
        ),
        out_specs=(P(("row", "col"), None, None), P(), P()),
        check_vma=False,
    )
```

time: 81.9 us -> 73.8 us (0.901)
  Pallas kernels: 77.6 us -> 72.2 us
  local copies, waits for them, and re-layouts: 2.71 us -> 0 us
    pallas_call x1, Pallas kernels: 77.6 us -> 70.8 us  [local(): pl.pallas_call(kernel, out_shape=(jax.ShapeDtypeStruct((2, STATES, TILE),...]
    unnamed x7 -> x0, local copies, waits for them, and re-layouts: 2.71 us -> none
    pallas_call x0 -> x1, Pallas kernels: none -> 1.4 us  [local(): pl.pallas_call(hand_on, out_shape=tuple((jax.ShapeDtypeStruct(r.shape, F3...]
where the time goes in v2:
time: 73.8 us; the launch traced here: 73.5 us
  Pallas kernels  72.2 us (98%)
  between operations  1.29 us (2%)
    pallas_call x1, Pallas kernels, local(): pl.pallas_call(kernel, out_shape=(jax.ShapeDtypeStruct((2, STATES, TILE),...  70.8 us

profile of v2, /device:TPU:1, one launch (start us, length us, event | category | flops | bytes accessed | tf_op | source)
XLA Modules:
  0.0 73.5 jit_solution(10516414253145327102)
XLA Ops:
  1.3 70.8 %shard_map.85 = (f32[2,16,256]{2,1,0:T(8,128)}, f32[16,16]{1,0:T(8,128)}, f32[32,32]{1,0:T(8,128)}) custom-call(bf16[1,1,6,256,256]{4,3,2,1,0:T(8,128)(2,1)} %tiles.1, s32[1,1,6]{2,1,0:T(1,128)} %rows.1, s32[1,1,6]{2,1,0:T(1,128)} %cols.1, s32[1,1]{1,0:T(1,128)S(6)} %copy.9.count, f32[2,16,256]{2,1,0:T(8,128)} %trial.1, f32[2,16,256]{2,1,0:T(8,128)} %search.1), custom_call_target="tpu_custom_call" | custom-call | tf_op jit(solution)/shard_map/pallas_call | solution.py:297
  72.1 1.4 %shard_map.86 = (f32[2,16,256]{2,1,0:T(8,128)}, f32[16,16]{1,0:T(8,128)}, f32[32,32]{1,0:T(8,128)}) custom-call(f32[2,16,256]{2,1,0:T(8,128)} %get-tuple-element.6.a, f32[16,16]{1,0:T(8,128)} %get-tuple-element.7.b, f32[32,32]{1,0:T(8,128)} %get-tuple-element.8.c), custom_call_target="tpu_custom_call" | custom-call | tf_op jit(solution)/shard_map/pallas_call | solution.py:329

commit v3 on v2

--- a/solution.py
+++ b/solution.py
@@ -33,11 +33,12 @@
 
 class Ring:
     def __init__(self, sems, at, peer, far_up):
-        self.sems, self.at, self.peer, self.far_up = sems, at, peer, far_up
-
-    def first(self):
+        self.sems, self.at, self.peer, self.far_up, self.c = sems, at, peer, far_up, {}
+
+    def first(self, distances=(2, -2, 1, -1)):
         own = self.at(0)
-        self.c = {d: self.sems.copy(own, own, self.peer(d)) for d in (2, -2, 1, -1)}
+        for d in distances:
+            self.c[d] = self.sems.copy(own, own, self.peer(d))
 
     def second(self):
         for sign in (1, -1):
@@ -53,9 +54,8 @@
 
 
 class Direct(Ring):
-    def first(self):
-        own = self.at(0)
-        self.c = {d: self.sems.copy(own, own, self.peer(d)) for d in (4, 3, -3, 2, -2, 1, -1)}
+    def first(self, distances=(4, 3, -3, 2, -2, 1, -1)):
+        Ring.first(self, distances)
 
     def second(self):
         pass
@@ -182,34 +182,38 @@
         rings_c[d].second()
     for d in (1, 3):
         rings_r[d].second()
-    ar0 = group_start(ar0y, yc, y_peer, y_order, group_sum(ar0x, ar0, 8))
     pad = jnp.zeros((8, 32, TILE), BF16)
     con_r[:, 96:, :] = pad
     con_c[:, 96:, :] = pad
     fetch.wait()
+
+    def con_ring(buf, me, peer, piece, far_up):
+        def at(off):
+            return buf.at[(me + off + 8) % 8, pl.ds(piece * 32, 32)]
+        return Ring(sems, at, peer, far_up)
+
+    out_r = [con_ring(con_r, x, x_peer, i, i != 1) for i in range(3)]
+    out_c = [con_ring(con_c, z, z_peer, i, i == 1) for i in range(3)]
     for d in (0, 1, 2, 3):
         rings_c[d].last()
-    for d in (0, 1, 3, 2):
-        rings_r[d].last()
-
-    def con_ring(buf, me, peer, half):
-        def at(off):
-            return buf.at[(me + off + 8) % 8, pl.ds(half * 48, 48)]
-        return Ring(sems, at, peer, half == 0)
-
-    out_r = [con_ring(con_r, x, x_peer, h) for h in range(2)]
-    out_c = [con_ring(con_c, z, z_peer, h) for h in range(2)]
     for s in range(SLOTS):
         product = lax.dot_general(gath_c[col_at[s]], tile_buf[s], NT, preferred_element_type=F32) * live[s]
         con_r[x, pl.ds(s * 16, 16), :] = product.astype(BF16)
-        if s % 3 == 2:
-            out_r[s // 3].first()
+        if s % 2 == 1:
+            out_r[s // 2].first((2, -2))
+    for ring in out_r:
+        ring.first((1, -1))
+    ar0 = group_start(ar0y, yc, y_peer, y_order, group_sum(ar0x, ar0, 8))
+    for d in (0, 1, 3, 2):
+        rings_r[d].last()
     for s in range(SLOTS):
         product = lax.dot_general(gath_r[row_at[s]], tile_buf[s], NN, preferred_element_type=F32) * live[s]
         con_c[z, pl.ds(s * 16, 16), :] = product.astype(BF16)
-        if s % 3 == 2:
-            out_c[s // 3].first()
-    for ring in (out_r[0], out_r[1], out_c[0], out_c[1]):
+        if s % 2 == 1:
+            out_c[s // 2].first((2, -2))
+    for ring in out_c:
+        ring.first((1, -1))
+    for ring in out_r + out_c:
         ring.second()
     ar0 = group_start(ar0z, z, z_peer, ring_order, group_sum(ar0y, ar0, 16))
     for c in codes:
@@ -234,6 +238,17 @@
     parts = reduce_first(con_r, code_r, out_r, x, yh, acc_r, low_r, part_r, h_peer)
     parts = parts + reduce_first(con_c, code_c, out_c, z, al, acc_c, low_c, part_c, l_peer)
 
+    pack[...] = jnp.zeros(pack.shape, F32)
+    for c in parts:
+        c.wait_recv()
+    image = acc_r[yh] + acc_c[al]
+    for i in range(3):
+        image = image + part_r[i].astype(F32) + part_c[i].astype(F32)
+    image_cat = jnp.concatenate([image[0:16], image[16:32]], axis=1)
+    stack = jnp.concatenate([trial_cat, image_cat, search_cat], axis=0)
+    pack[0:16, 0:48] = lax.dot_general(image_cat, stack, NT, precision=HI, preferred_element_type=F32)
+    step = group_start(ar1x, x, x_peer, ring_order, pack_rows(pack, 16, 64))
+
     total = group_sum(ar0z, ar0, 8) / BASIS
     known[0:16] = jnp.concatenate([total, pltpu.roll(total, 96, 1)], axis=0)
     known[16:32] = jnp.concatenate([pltpu.roll(total, 64, 1), pltpu.roll(total, 32, 1)], axis=0)
@@ -246,18 +261,10 @@
         work = jnp.where(row_id == j, pivot, work - work[:, j:j + 1] * pivot)
     pack[0:16, :] = work
     inverse = pack[0:16, 16:32]
+    solved = lax.dot_general(inverse, trial_cat, NN, precision=HI, preferred_element_type=F32)
+    side_solved = lax.dot_general(
+        inverse, known[0:16, 16:32], NN, precision=HI, preferred_element_type=F32)
     gram[16:32, 16:32] = known[16:32, 16:32]
-    pack[...] = jnp.zeros(pack.shape, F32)
-    for c in parts:
-        c.wait_recv()
-    image = acc_r[yh] + acc_c[al]
-    for i in range(3):
-        image = image + part_r[i].astype(F32) + part_c[i].astype(F32)
-    image_cat = jnp.concatenate([image[0:16], image[16:32]], axis=1)
-    stack = jnp.concatenate([trial_cat, image_cat, search_cat], axis=0)
-    pack[0:16, 0:48] = lax.dot_general(image_cat, stack, NT, precision=HI, preferred_element_type=F32)
-    step = group_start(ar1x, x, x_peer, ring_order, pack_rows(pack, 16, 64))
-
     step = group_start(ar1y, yc, y_peer, y_order, group_sum(ar1x, step, 8))
     step = group_start(ar1z, z, z_peer, ring_order, group_sum(ar1y, step, 16))
     total = group_sum(ar1z, step, 8) / BASIS
@@ -265,14 +272,14 @@
     pack[0:16, :] = jnp.concatenate([total, pltpu.roll(total, 64, 1)], axis=0)
     mixed = pack[0:16, 0:16]
     turned = lax.dot_general(mixed, inverse, NN, precision=HI, preferred_element_type=F32)
-    fixed = lax.dot_general(turned, trial_cat, NN, precision=HI, preferred_element_type=F32)
+    fixed = lax.dot_general(mixed, solved, NN, precision=HI, preferred_element_type=F32)
     residual[0] = image[0:16] - fixed[:, 0:TILE]
     residual[1] = image[16:32] - fixed[:, TILE:]
     rayleigh[...] = lax.dot_general(inverse, mixed, NT, precision=HI, preferred_element_type=F32)
     gram[0:16, 0:16] = pack[0:16, 16:32] - lax.dot_general(
         turned, mixed, NT, precision=HI, preferred_element_type=F32)
     side = pack[0:16, 32:48] - lax.dot_general(
-        turned, known[0:16, 16:32], NN, precision=HI, preferred_element_type=F32)
+        mixed, side_solved, NN, precision=HI, preferred_element_type=F32)
     gram[0:16, 16:32] = side
     gram[16:32, 0:16] = lax.dot_general(
         ident[:, 0:16], side, NT, precision=HI, preferred_element_type=F32)
@@ -288,7 +295,7 @@
 
 
 BASIS = 524288.0
-COPIES = 168
+COPIES = 182
 
 
 def local(tiles, tile_rows, tile_cols, tile_counts, trial, search):
@@ -297,9 +304,9 @@
     results = pl.pallas_call(
         kernel,
         out_shape=(
-            jax.ShapeDtypeStruct((2, STATES, TILE), F32),
-            jax.ShapeDtypeStruct((STATES, STATES), F32),
-            jax.ShapeDtypeStruct((2 * STATES, 2 * STATES), F32),
+            pltpu.VMEM((2, STATES, TILE), F32),
+            pltpu.VMEM((STATES, STATES), F32),
+            pltpu.VMEM((2 * STATES, 2 * STATES), F32),
         ),
         in_specs=[pl.BlockSpec(memory_space=pl.ANY), smem, smem, vmem, vmem, vmem],
         out_specs=(vmem, vmem, vmem),
@@ -331,7 +338,7 @@
         out_shape=tuple(jax.ShapeDtypeStruct(r.shape, F32) for r in results),
         in_specs=[vmem] * 3,
         out_specs=(vmem,) * 3,
-    )(*results)
+    )(*[pltpu.with_memory_space_constraint(r, pltpu.VMEM) for r in results])
 
 
 def solution(mesh):

time: 73.8 us -> 71.2 us (0.965)
  Pallas kernels: 72.2 us -> 69.7 us
    pallas_call x1, Pallas kernels: 70.8 us -> 69.1 us  [local(): pl.pallas_call(kernel, out_shape=(pltpu.VMEM((2, STATES, TILE), F32), plt...]
    pallas_call x1, Pallas kernels: 1.4 us -> 0.63 us  [local(): pl.pallas_call(hand_on, out_shape=tuple((jax.ShapeDtypeStruct(r.shape, F3...]
where the time goes in v3:
time: 71.2 us; the launch traced here: 71 us
  Pallas kernels  69.7 us (98%)
  between operations  1.29 us (2%)
    pallas_call x1, Pallas kernels, local(): pl.pallas_call(kernel, out_shape=(pltpu.VMEM((2, STATES, TILE), F32), plt...  69.1 us

profile of v3, /device:TPU:1, one launch (start us, length us, event | category | flops | bytes accessed | tf_op | source)
XLA Modules:
  0.0 71.0 jit_solution(55604746104050791)
XLA Ops:
  1.3 69.1 %shard_map.85 = (f32[2,16,256]{2,1,0:T(8,128)S(1)}, f32[16,16]{1,0:T(8,128)S(1)}, f32[32,32]{1,0:T(8,128)S(1)}) custom-call(bf16[1,1,6,256,256]{4,3,2,1,0:T(8,128)(2,1)} %tiles.1, s32[1,1,6]{2,1,0:T(1,128)} %rows.1, s32[1,1,6]{2,1,0:T(1,128)} %cols.1, s32[1,1]{1,0:T(1,128)S(6)} %copy.9.count, f32[2,16,256]{2,1,0:T(8,128)} %trial.1, f32[2,16,256]{2,1,0:T(8,128)} %search.1), custom_call_target="tpu_custom_call" | custom-call | tf_op jit(solution)/shard_map/pallas_call | solution.py:304
  70.4 0.6 shard_map.86

commit v4 on v3

--- a/solution.py
+++ b/solution.py
@@ -72,9 +72,9 @@
     return total
 
 
-def kernel(tiles, rows, cols, count, trial, search, residual, rayleigh, gram,
+def kernel(tiles, rows_in, cols_in, count_in, trial_in, search_in, residual, rayleigh, gram,
            tile_buf, gath_r, gath_c, con_r, con_c, code_r, code_c, acc_r, acc_c, low_r, low_c, part_r, part_c,
-           ar0x, ar0y, ar0z, ar1x, ar1y, ar1z, pack, known, tile_sem, send, recv):
+           trial, search, rows, cols, count, in_sem, ar0x, ar0y, ar0z, ar1x, ar1y, ar1z, pack, known, tile_sem, send, recv):
     p, q = lax.axis_index("row"), lax.axis_index("col")
     x, yh = q // 4, q % 4
     yl, z, core = p // 16, (p // 2) % 8, p % 2
@@ -105,20 +105,19 @@
     barrier = pltpu.get_barrier_semaphore()
     for peer in [x_peer(d) for d in ring_order] + [z_peer(d) for d in ring_order] + [y_peer(d) for d in y_order]:
         pl.semaphore_signal(barrier, inc=1, device_id=peer, device_id_type=MESH)
+    loads = [pltpu.make_async_copy(src, dst, in_sem.at[i]) for i, (src, dst) in enumerate((
+        (trial_in, trial), (search_in, search), (rows_in, rows), (cols_in, cols), (count_in, count)))]
+    for load in loads:
+        load.start()
     fetch = pltpu.make_async_copy(tiles.at[0, 0], tile_buf, tile_sem)
     fetch.start()
+    loads[0].wait()
 
     low = trial[...].astype(BF16)
     own_r = pl.ds(pl.multiple_of(x * 8 + yh * 2, 2), 2)
     own_c = pl.ds(pl.multiple_of(z * 8 + al * 2, 2), 2)
     gath_r[own_r] = low
     gath_c[own_c] = low
-
-    trial_cat = jnp.concatenate([trial[0], trial[1]], axis=1)
-    search_cat = jnp.concatenate([search[0], search[1]], axis=1)
-    held = jnp.concatenate([trial_cat, search_cat], axis=0)
-    pack[...] = jnp.zeros(pack.shape, F32)
-    pack[:, 0:32] = lax.dot_general(held, held, NT, precision=HI, preferred_element_type=F32)
 
     pl.semaphore_wait(barrier, 29)
 
@@ -147,7 +146,14 @@
     group_c = {d: sems.copy(gath_c.at[own_c], gath_c.at[own_c], l_peer(d)) for d in (2, 1, 3)}
     rings_c[0].first()
 
-    used = count[...]
+    for load in loads[1:]:
+        load.wait()
+    trial_cat = jnp.concatenate([trial[0], trial[1]], axis=1)
+    search_cat = jnp.concatenate([search[0], search[1]], axis=1)
+    held = jnp.concatenate([trial_cat, search_cat], axis=0)
+    pack[...] = jnp.zeros(pack.shape, F32)
+    pack[:, 0:32] = lax.dot_general(held, held, NT, precision=HI, preferred_element_type=F32)
+    used = count[0, 0]
     row_at, col_at, live = [], [], []
     for s in range(SLOTS):
         i, j = rows[0, 0, s], cols[0, 0, s]
@@ -265,6 +271,9 @@
     side_solved = lax.dot_general(
         inverse, known[0:16, 16:32], NN, precision=HI, preferred_element_type=F32)
     gram[16:32, 16:32] = known[16:32, 16:32]
+    sent = len(sems.copies)
+    for c in sems.copies:
+        c.wait_send()
     step = group_start(ar1y, yc, y_peer, y_order, group_sum(ar1x, step, 8))
     step = group_start(ar1z, z, z_peer, ring_order, group_sum(ar1y, step, 16))
     total = group_sum(ar1z, step, 8) / BASIS
@@ -284,7 +293,7 @@
     gram[16:32, 0:16] = lax.dot_general(
         ident[:, 0:16], side, NT, precision=HI, preferred_element_type=F32)
 
-    for c in sems.copies:
+    for c in sems.copies[sent:]:
         c.wait_send()
 
 
@@ -299,7 +308,6 @@
 
 
 def local(tiles, tile_rows, tile_cols, tile_counts, trial, search):
-    smem = pl.BlockSpec(memory_space=pltpu.SMEM)
     vmem = pl.BlockSpec(memory_space=pltpu.VMEM)
     results = pl.pallas_call(
         kernel,
@@ -308,7 +316,7 @@
             pltpu.VMEM((STATES, STATES), F32),
             pltpu.VMEM((2 * STATES, 2 * STATES), F32),
         ),
-        in_specs=[pl.BlockSpec(memory_space=pl.ANY), smem, smem, vmem, vmem, vmem],
+        in_specs=[pl.BlockSpec(memory_space=pl.ANY)] * 6,
         out_specs=(vmem, vmem, vmem),
         scratch_shapes=[
             pltpu.VMEM((SLOTS, TILE, TILE), BF16),
@@ -324,6 +332,12 @@
             pltpu.VMEM((4, 32, TILE), BF16),
             pltpu.VMEM((3, 32, TILE), BF16),
             pltpu.VMEM((3, 32, TILE), BF16),
+            pltpu.VMEM((2, STATES, TILE), F32),
+            pltpu.VMEM((2, STATES, TILE), F32),
+            pltpu.SMEM((1, 1, SLOTS), jnp.int32),
+            pltpu.SMEM((1, 1, SLOTS), jnp.int32),
+            pltpu.SMEM((1, 1), jnp.int32),
+            pltpu.SemaphoreType.DMA((5,)),
         ] + [pltpu.VMEM((n, 8, 128), F32) for n in (8, 16, 8, 8, 16, 8)] + [
             pltpu.VMEM((32, 128), F32),
             pltpu.VMEM((32, 128), F32),

time: 71.2 us -> 70.2 us (0.986)
  Pallas kernels: 69.7 us -> 68.7 us
    pallas_call x1, Pallas kernels: 69.1 us -> 68.1 us  [local(): pl.pallas_call(kernel, out_shape=(pltpu.VMEM((2, STATES, TILE), F32), plt...]
where the time goes in v4:
time: 70.2 us; the launch traced here: 70 us
  Pallas kernels  68.7 us (98%)
  between operations  1.29 us (2%)
    pallas_call x1, Pallas kernels, local(): pl.pallas_call(kernel, out_shape=(pltpu.VMEM((2, STATES, TILE), F32), plt...  68.1 us

profile of v4, /device:TPU:1, one launch (start us, length us, event | category | flops | bytes accessed | tf_op | source)
XLA Modules:
  0.0 70.0 jit_solution(4310358512714339031)
XLA Ops:
  1.3 68.1 %shard_map.85 = (f32[2,16,256]{2,1,0:T(8,128)S(1)}, f32[16,16]{1,0:T(8,128)S(1)}, f32[32,32]{1,0:T(8,128)S(1)}) custom-call(bf16[1,1,6,256,256]{4,3,2,1,0:T(8,128)(2,1)} %tiles.1, s32[1,1,6]{2,1,0:T(1,128)} %rows_in.1, s32[1,1,6]{2,1,0:T(1,128)} %cols_in.1, s32[1,1]{1,0:T(1,128)S(6)} %copy.9.count_in, f32[2,16,256]{2,1,0:T(8,128)} %trial_in.1, ...), custom_call_target="tpu_custom_call" | custom-call | tf_op jit(solution)/shard_map/pallas_call | solution.py:312
  69.4 0.6 shard_map.86
